TPU v7x, 32 devices: a whole 2x2x4 slice. The times are simulated.
32 devices in a mesh: groups: 2 (over x), ctx: 16 (over z, y, core).
Axes of the slice: x: 2, y: 2, z: 4, core: 2. Of those that a mesh axis runs over, the one named last changes fastest.
Arguments:
- queries: bfloat16 [16384, 1024], P(('groups', 'ctx')), parts along dimension 0, may hold values from -24 to 24
- key_rows: bfloat16 [16384, 1024], P(('groups', 'ctx')), parts along dimension 0, may hold values from -12 to 12
- value_rows: bfloat16 [16384, 1024], P(('groups', 'ctx')), parts along dimension 0, may hold values from -6 to 6
- step_rates: float32 [2, 16384], P(None, ('groups', 'ctx')), parts along dimension 1, may hold values from 0.002 to 0.02
- w_gate: bfloat16 [2048, 512], P('groups'), parts along dimension 0, may hold values from -2 to 2
- w_up: bfloat16 [2048, 512], P('groups'), parts along dimension 0, may hold values from -2 to 2
- w_down: bfloat16 [2048, 512], P('groups'), parts along dimension 0, may hold values from -2 to 2
Outputs:
- layer_out: bfloat16 [16384, 1024], P(('groups', 'ctx')), parts along dimension 0
- new_weights: bfloat16 [6144, 512], P(('groups', 'ctx')), parts along dimension 0
There are 2 independent parts, one for each index of `groups`. A program takes and returns all parts, laid end to end along the dimension named above; each array names one. Nothing has to cross between parts.
All inputs are finite; a program needn't handle non-finite values.
Results may differ from a plain program's by a relative error of at most 0.012.
The roundings to bfloat16 on the way count: a program that leaves them out, or rounds other values in their place, can miss the bound.
Values may be sent and summed in bfloat16 or wider, within the bound.
No kernel may reach another device: no remote copies, remote signals or barrier semaphores. Data moves between devices by JAX's collectives and lax.ppermute only.
A program may use at most 64 MiB of HBM per device.

v0:
```python
import math
import jax
import jax.numpy as jnp
from jax import lax
from jax.sharding import PartitionSpec as P

H = 2
HD = 512
WINDOW = 1024


def passed_along(value, axis, steps):
    count = lax.axis_size(axis)
    leading, last = (max(0, -steps), min(count, count - steps))
    return lax.ppermute(value, axis, [(source, source + steps) for source in range(leading, last)])


def rms_rows(row_values):
    values = row_values.astype(jnp.float32).reshape(row_values.shape[0], H, HD)
    return (values * lax.rsqrt(jnp.mean(values * values, -1, keepdims=True) + 1e-06)).astype(
        jnp.bfloat16
    )


def normalize_rows(old_rows, grad_rows):
    old_values = old_rows.astype(jnp.float32)
    raised = old_values - grad_rows
    factor = jnp.sqrt(jnp.mean(old_values * old_values, -1, keepdims=True) + 1e-06) * lax.rsqrt(
        jnp.mean(raised * raised, -1, keepdims=True) + 1e-06
    )
    return (raised * factor).astype(jnp.bfloat16)


def local(queries, key_rows, value_rows, step_rates, w_gate, w_up, w_down):
    tok_rows = queries.shape[0]
    reach = WINDOW // tok_rows
    earlier_keys = []
    earlier_values = []
    for step in range(reach, 0, -1):
        moved = passed_along((key_rows, value_rows), "ctx", step)
        earlier_keys.append(moved[0])
        earlier_values.append(moved[1])
    all_keys = jnp.concatenate(earlier_keys + [key_rows], 0)
    all_values = jnp.concatenate(earlier_values + [value_rows], 0)
    own_start = lax.axis_index("ctx") * tok_rows
    block_rows = min(512, tok_rows)
    q_block = queries.reshape(block_rows, H, HD)
    k_block = all_keys.reshape(WINDOW + block_rows, H, HD)
    v_block = all_values.reshape(WINDOW + block_rows, H, HD)
    scores = jnp.einsum("qhd,khd->hqk", q_block, k_block, preferred_element_type=jnp.float32) * (
        1.0 / math.sqrt(HD)
    )
    q_pos = 0 + jnp.arange(block_rows, dtype=jnp.int32)
    k_pos = 0 - WINDOW + jnp.arange(WINDOW + block_rows, dtype=jnp.int32)
    allowed = (
        (k_pos[None, :] <= q_pos[:, None])
        & (k_pos[None, :] > q_pos[:, None] - WINDOW)
        & (k_pos[None, :] + own_start >= 0)
    )
    scores = jnp.where(allowed[None], scores, -jnp.inf)
    highest = jnp.max(scores, -1, keepdims=True)
    expo = jnp.exp(scores - highest)
    weights = (expo / jnp.sum(expo, -1, keepdims=True)).astype(jnp.bfloat16)
    result = jnp.einsum("hqk,khd->qhd", weights, v_block, preferred_element_type=jnp.float32)
    pieces = result.astype(jnp.bfloat16)
    q_norm = rms_rows(queries)
    k_norm = rms_rows(key_rows)
    gate_m = w_gate.reshape(H, HD, HD)
    up_m = w_up.reshape(H, HD, HD)
    down_m = w_down.reshape(H, HD, HD)
    pre_gate = jnp.einsum("thd,hjd->thj", k_norm, gate_m, preferred_element_type=jnp.float32)
    pre_up = jnp.einsum("thd,hjd->thj", k_norm, up_m, preferred_element_type=jnp.float32)
    sig = jax.nn.sigmoid(pre_gate)
    active = pre_gate * sig
    gated = (active * pre_up).astype(jnp.bfloat16)
    errors = (-step_rates.T[:, :, None] * pieces.astype(jnp.float32)).astype(jnp.bfloat16)
    grad_down = jnp.einsum("tho,thj->hoj", errors, gated, preferred_element_type=jnp.float32)
    back = jnp.einsum("tho,hoj->thj", errors, down_m, preferred_element_type=jnp.float32)
    d_gate = (back * pre_up * sig * (1.0 + pre_gate * (1.0 - sig))).astype(jnp.bfloat16)
    d_up = (back * active).astype(jnp.bfloat16)
    grad_gate = jnp.einsum("thj,thd->hjd", d_gate, k_norm, preferred_element_type=jnp.float32)
    grad_up = jnp.einsum("thj,thd->hjd", d_up, k_norm, preferred_element_type=jnp.float32)
    grads = jnp.concatenate(
        [grad_gate.reshape(H * HD, HD), grad_up.reshape(H * HD, HD), grad_down.reshape(H * HD, HD)],
        0,
    )
    old_rows = jnp.concatenate([w_gate, w_up, w_down], 0)
    own_count = grads.shape[0] // lax.axis_size("ctx")
    own_first = lax.axis_index("ctx") * own_count
    summed = lax.psum(grads, "ctx")
    fresh = normalize_rows(old_rows, summed)
    own_weights = lax.dynamic_slice_in_dim(fresh, own_first, own_count, 0)
    new_gate = fresh[: H * HD].reshape(H, HD, HD)
    new_up = fresh[H * HD : 2 * H * HD].reshape(H, HD, HD)
    new_down = fresh[2 * H * HD :].reshape(H, HD, HD)
    q_gate = jnp.einsum("thd,hjd->thj", q_norm, new_gate, preferred_element_type=jnp.float32)
    q_up = jnp.einsum("thd,hjd->thj", q_norm, new_up, preferred_element_type=jnp.float32)
    q_gated = (q_gate * jax.nn.sigmoid(q_gate) * q_up).astype(jnp.bfloat16)
    fast_out = jnp.einsum("thj,hoj->tho", q_gated, new_down, preferred_element_type=jnp.float32)
    layer_out = (
        (pieces.astype(jnp.float32) + fast_out).astype(jnp.bfloat16).reshape(tok_rows, H * HD)
    )
    return (layer_out, own_weights)


def solution(mesh):
    return jax.shard_map(
        local,
        mesh=mesh,
        in_specs=(
            P(("groups", "ctx"), None),
            P(("groups", "ctx"), None),
            P(("groups", "ctx"), None),
            P(None, ("groups", "ctx")),
            P("groups", None),
            P("groups", None),
            P("groups", None),
        ),
        out_specs=(P(("groups", "ctx"), None), P(("groups", "ctx"), None)),
        check_vma=False,
    )
```

profile of v0, /device:TPU:0, one launch (start us, length us, event | category | flops | bytes accessed | tf_op | source)
XLA Modules:
  0.0 283.9 jit_solution(13785161849252597991)
XLA Ops:
  8.7 5.9 %collective-permute-start.2 = (bf16[512,1024]{0,1:T(8,128)(2,1)S(1)}, bf16[512,1024]{0,1:T(8,128)(2,1)}, u32[]{:S(2)}, u32[]{:S(2)}) collective-permute-start(bf16[512,1024]{0,1:T(8,128)(2,1)S(1)} %copy.89), channel_id=1, source_target_pairs={{0,2},{1,3},{2,4},{3,5},{4,6},{5,7},{6,8},{7,9},{8,10},{9,11},{10,... | collective-permute-start | bytes 3145736 | tf_op jit(solution)/shard_map/ppermute | solution.py:15
  14.6 2.4 collective-permute-start.3
  17.0 3.0 %collective-permute-start = (bf16[512,1024]{1,0:T(8,128)(2,1)}, bf16[512,1024]{1,0:T(8,128)(2,1)}, u32[]{:S(2)}, u32[]{:S(2)}) collective-permute-start(bf16[512,1024]{1,0:T(8,128)(2,1)} %param.9), channel_id=1, source_target_pairs={{0,2},{1,3},{2,4},{3,5},{4,6},{5,7},{6,8},{7,9},{8,10},{9,11},{10,... | collective-permute-start | bytes 3145736 | tf_op jit(solution)/shard_map/ppermute | solution.py:15
  20.0 4.2 %collective-permute-start.1 = (bf16[512,1024]{1,0:T(8,128)(2,1)}, bf16[512,1024]{1,0:T(8,128)(2,1)}, u32[]{:S(2)}, u32[]{:S(2)}) collective-permute-start(bf16[512,1024]{1,0:T(8,128)(2,1)} %param.9), channel_id=1, source_target_pairs={{0,1},{1,2},{2,3},{3,4},{4,5},{5,6},{6,7},{7,8},{8,9},{9,10},{10,1... | collective-permute-start | bytes 3145736 | tf_op jit(solution)/shard_map/ppermute | solution.py:15
  24.5 1.6 copy.99
  26.1 1.9 multiply_convert_fusion.1
  28.0 2.2 fusion.59
  30.2 2.1 fusion.58
  32.3 2.0 fusion.7
  34.3 25.5 %collective-permute-done = bf16[512,1024]{1,0:T(8,128)(2,1)} collective-permute-done((bf16[512,1024]{1,0:T(8,128)(2,1)}, bf16[512,1024]{1,0:T(8,128)(2,1)}, u32[]{:S(2)}, u32[]{:S(2)}) %collective-permute-start) | collective-permute-done | bytes 1048608 | tf_op jit(solution)/shard_map/ppermute | solution.py:15
  59.7 3.0 %pad_maximum_fusion.1 = bf16[1536,1024]{1,0:T(8,128)(2,1)} fusion(bf16[512,1024]{1,0:T(8,128)(2,1)S(1)} %copy-done.14, bf16[512,1024]{1,0:T(8,128)(2,1)} %collective-permute-done.1, bf16[512,1024]{1,0:T(8,128)(2,1)} %collective-permute-done), kind=kLoop, calls=%fused_computation.11 | loop fusion | flops 9437184 | bytes 6291456 | tf_op jit(solution)/shard_map/concatenate | solution.py:44
  62.8 4.7 %copy.88 = bf16[1536,1024]{0,1:T(8,128)(2,1)} copy(bf16[1536,1024]{1,0:T(8,128)(2,1)} %pad_maximum_fusion.1) | data formatting | bytes 6291456 | tf_op jit(solution)/shard_map/concatenate | solution.py:44
  67.5 1.9 pad_maximum_fusion.2
  69.4 2.4 fusion.31
  71.9 2.2 fusion.57
  74.5 7.7 %fusion.26 = bf16[2,512,512]{2,1,0:T(8,128)(2,1)} fusion(bf16[1536,2,512]{0,2,1:T(8,128)(2,1)} %bitcast.136, f32[2,512]{1,0:T(2,128)S(1)} %fusion.57, f32[2,1536,512]{2,1,0:T(8,128)} %copy-done.10, pred[512,1536]{0,1:T(8,128)(4,1)} %fusion.7), kind=kOutput, calls=%fused_computation.53 | convolution fusion | flops 1619003904 | bytes 11276288 | tf_op jit(solution)/shard_map/hqk,khd->qhd/dot_general | solution.py:64
  82.3 2.1 fusion.36
  88.2 3.4 %pad_maximum_fusion = f32[3072,512]{1,0:T(8,128)} fusion(f32[1024,512]{1,0:T(8,128)S(1)} %bitcast.139, f32[1024,512]{1,0:T(8,128)S(1)} %bitcast.137, f32[1024,512]{1,0:T(8,128)S(1)} %bitcast.138), kind=kLoop, calls=%fused_computation.4 | loop fusion | flops 3145728 | bytes 12582912 | tf_op jit(solution)/shard_map/concatenate | solution.py:83
  91.9 162.4 %all-reduce.2.cloned.1.call-done = f32[3072,512]{1,0:T(8,128)} async-done(((f32[3072,512]{1,0:T(8,128)}), f32[3072,512]{1,0:T(8,128)}) %all-reduce.2.cloned.1.call-update) | async-done | bytes 6291472 | tf_op jit(solution)/shard_map/psum | solution.py:90
  254.3 4.4 %fusion.1 = (f32[3072]{0:T(1024)S(1)}, f32[3072]{0:T(1024)S(1)}) fusion(bf16[1024,512]{1,0:T(8,128)(2,1)S(1)} %copy-done.3, bf16[1024,512]{1,0:T(8,128)(2,1)S(1)} %copy-done.6, bf16[1024,512]{1,0:T(8,128)(2,1)} %param.11, f32[3072,512]{1,0:T(8,128)} %all-reduce.2.cloned.1.call-done), kind=kLoop, calls=%fused_computation.3 | loop fusion | flops 17295360 | bytes 9461760 | tf_op jit(solution)/shard_map/reduce_sum | solution.py:28
  260.1 5.1 %multiply_convert_fusion = bf16[3072,512]{1,0:T(8,128)(2,1)S(1)} fusion(f32[3072,512]{1,0:T(8,128)S(1)} %copy-done, f32[3072]{0:T(1024)S(1)} %rsqrt_multiply_fusion, bf16[1024,512]{1,0:T(8,128)(2,1)S(1)} %copy-done.4, bf16[1024,512]{1,0:T(8,128)(2,1)S(1)} %copy-done.7, bf16[1024,512]{1,0:T(8,128)(2,1)S(1)} %copy-done.9), kind=kLoop, calls=%fused_computation.6 | loop fusion | flops 14155776 | bytes 12595200 | tf_op jit(solution)/shard_map/convert_element_type | solution.py:31
  266.7 2.1 fusion.40
  268.8 5.3 %fusion.11 = bf16[512,2,512]{0,2,1:T(8,128)(2,1)} fusion(bf16[2,512,512]{2,1,0:T(8,128)(2,1)} %fusion.26, bf16[2,512,512]{2,1,0:T(8,128)(2,1)} %bitcast.142, f32[2,512,512]{1,2,0:T(8,128)} %fusion.40, bf16[2,512,512]{2,1,0:T(8,128)(2,1)} %bitcast.141, f32[512,2]{0,1:T(2,128)S(1)} %add_rsqrt_fusion, bf16[64,2,8,512]{3,2,1,0:T(8,128)(2,1)} %bitcast.128), kind=kOutput, calls=%fused_computation.26 | convolution fusion | flops 1080033280 | bytes 7344128 | tf_op jit(solution)/shard_map/thj,hoj->tho/dot_general | solution.py:99
  274.1 2.3 copy.105
  (54 shorter events, 9.9 us)
Async XLA Ops:
  7.2 247.1 %all-reduce.2.cloned.1.call-start = ((), (), s32[]{:S(2)}) async-start(), calls=%async_computation | async-start | bytes 12582912 | tf_op jit(solution)/shard_map/psum | solution.py:90
  8.7 58.8 %collective-permute-start.2 = (bf16[512,1024]{0,1:T(8,128)(2,1)S(1)}, bf16[512,1024]{0,1:T(8,128)(2,1)}, u32[]{:S(2)}, u32[]{:S(2)}) collective-permute-start(bf16[512,1024]{0,1:T(8,128)(2,1)S(1)} %copy.89), channel_id=1, source_target_pairs={{0,2},{1,3},{2,4},{3,5},{4,6},{5,7},{6,8},{7,9},{8,10},{9,11},{10,... | collective-permute-start | bytes 3145736 | tf_op jit(solution)/shard_map/ppermute | solution.py:15
  14.6 52.9 %collective-permute-start.3 = (bf16[512,1024]{0,1:T(8,128)(2,1)S(1)}, bf16[512,1024]{0,1:T(8,128)(2,1)}, u32[]{:S(2)}, u32[]{:S(2)}) collective-permute-start(bf16[512,1024]{0,1:T(8,128)(2,1)S(1)} %copy.89), channel_id=1, source_target_pairs={{0,1},{1,2},{2,3},{3,4},{4,5},{5,6},{6,7},{7,8},{8,9},{9,10},{10,1... | collective-permute-start | bytes 3145736 | tf_op jit(solution)/shard_map/ppermute | solution.py:15
  17.0 42.7 %collective-permute-start = (bf16[512,1024]{1,0:T(8,128)(2,1)}, bf16[512,1024]{1,0:T(8,128)(2,1)}, u32[]{:S(2)}, u32[]{:S(2)}) collective-permute-start(bf16[512,1024]{1,0:T(8,128)(2,1)} %param.9), channel_id=1, source_target_pairs={{0,2},{1,3},{2,4},{3,5},{4,6},{5,7},{6,8},{7,9},{8,10},{9,11},{10,... | collective-permute-start | bytes 3145736 | tf_op jit(solution)/shard_map/ppermute | solution.py:15
  20.0 39.8 %collective-permute-start.1 = (bf16[512,1024]{1,0:T(8,128)(2,1)}, bf16[512,1024]{1,0:T(8,128)(2,1)}, u32[]{:S(2)}, u32[]{:S(2)}) collective-permute-start(bf16[512,1024]{1,0:T(8,128)(2,1)} %param.9), channel_id=1, source_target_pairs={{0,1},{1,2},{2,3},{3,4},{4,5},{5,6},{6,7},{7,8},{8,9},{9,10},{10,1... | collective-permute-start | bytes 3145736 | tf_op jit(solution)/shard_map/ppermute | solution.py:15
  24.5 3.6 %copy-start.8 = (bf16[1024,512]{1,0:T(8,128)(2,1)S(1)}, bf16[1024,512]{1,0:T(8,128)(2,1)}, u32[]{:S(2)}) copy-start(bf16[1024,512]{1,0:T(8,128)(2,1)} %param.11) | copy-start | bytes 3145732
  26.1 4.1 %copy-start.5 = (bf16[1024,512]{1,0:T(8,128)(2,1)S(1)}, bf16[1024,512]{1,0:T(8,128)(2,1)}, u32[]{:S(2)}) copy-start(bf16[1024,512]{1,0:T(8,128)(2,1)} %param.12) | copy-start | bytes 3145732
  30.2 2.1 copy-start.16
  30.2 29.5 %copy-start.14 = (bf16[512,1024]{1,0:T(8,128)(2,1)S(1)}, bf16[512,1024]{1,0:T(8,128)(2,1)}, u32[]{:S(2)}) copy-start(bf16[512,1024]{1,0:T(8,128)(2,1)} %param.9) | copy-start | bytes 3145732
  67.5 1.9 copy-start.1
  69.4 2.4 copy-start.15
  71.9 2.6 copy-start.10
  74.5 7.8 %copy-start.3 = (bf16[1024,512]{1,0:T(8,128)(2,1)S(1)}, bf16[1024,512]{1,0:T(8,128)(2,1)}, u32[]{:S(2)}) copy-start(bf16[1024,512]{1,0:T(8,128)(2,1)} %param.13) | copy-start | bytes 3145732
  82.3 2.1 copy-start.11
  84.4 1.6 copy-start.12
  86.0 1.2 copy-start.13
  91.6 162.7 %copy-start.6 = (bf16[1024,512]{1,0:T(8,128)(2,1)S(1)}, bf16[1024,512]{1,0:T(8,128)(2,1)}, u32[]{:S(2)}) copy-start(bf16[1024,512]{1,0:T(8,128)(2,1)} %param.12) | copy-start | bytes 3145732
  254.3 4.9 %copy-start = (f32[3072,512]{1,0:T(8,128)S(1)}, f32[3072,512]{1,0:T(8,128)}, u32[]{:S(2)}) copy-start(f32[3072,512]{1,0:T(8,128)} %all-reduce.2.cloned.1.call-done) | copy-start | bytes 18874372
  254.3 5.2 %copy-start.4 = (bf16[1024,512]{1,0:T(8,128)(2,1)S(1)}, bf16[1024,512]{1,0:T(8,128)(2,1)}, u32[]{:S(2)}) copy-start(bf16[1024,512]{1,0:T(8,128)(2,1)} %param.13) | copy-start | bytes 3145732
  254.3 5.5 %copy-start.7 = (bf16[1024,512]{1,0:T(8,128)(2,1)S(1)}, bf16[1024,512]{1,0:T(8,128)(2,1)}, u32[]{:S(2)}) copy-start(bf16[1024,512]{1,0:T(8,128)(2,1)} %param.12) | copy-start | bytes 3145732
  254.3 5.8 %copy-start.9 = (bf16[1024,512]{1,0:T(8,128)(2,1)S(1)}, bf16[1024,512]{1,0:T(8,128)(2,1)}, u32[]{:S(2)}) copy-start(bf16[1024,512]{1,0:T(8,128)(2,1)} %param.11) | copy-start | bytes 3145732
  265.1 1.5 copy-start.2
Sparse Core Ops, SparseCore 0:
  91.7 162.5 all-reduce.1
where the time goes:
time: 284 us
  waiting for transfers between devices  188 us (66%)
  matrix products  26.9 us (9%)
  other arithmetic  24.4 us (9%)
  starting transfers between devices  15.5 us (5%)
  local copies, waits for them, and re-layouts  14.9 us (5%)
  between operations  14.2 us (5%)
    psum x1, waiting for transfers between devices, local(): summed = lax.psum(grads, 'ctx')  162 us
    ppermute x4, waiting for transfers between devices, passed_along(): lax.ppermute(value, axis, [(source, source + steps) for source in range(l...  25.5 us
    ppermute x4, starting transfers between devices, passed_along(): lax.ppermute(value, axis, [(source, source + steps) for source in range(l...  15.5 us
    dot_general x1, matrix products, local(): jnp.einsum('hqk,khd->qhd', weights, v_block, preferred_element_type=jnp.f...  7.75 us
    unnamed x36, local copies, waits for them, and re-layouts  6.35 us
  transfers between devices with their start and end apart: 5, of which 2 were waited for; matrix products, arithmetic and copies ran while one was open for 6% of the time, Pallas kernels for 0%

commit v1 on v0

--- a/solution.py
+++ b/solution.py
@@ -87,7 +87,9 @@
     old_rows = jnp.concatenate([w_gate, w_up, w_down], 0)
     own_count = grads.shape[0] // lax.axis_size("ctx")
     own_first = lax.axis_index("ctx") * own_count
-    summed = lax.psum(grads, "ctx")
+    summed = grads
+    for hop in (1, 2, 4, 8):
+        summed = summed + lax.ppermute(summed, "ctx", [(dev, dev ^ hop) for dev in range(16)])
     fresh = normalize_rows(old_rows, summed)
     own_weights = lax.dynamic_slice_in_dim(fresh, own_first, own_count, 0)
     new_gate = fresh[: H * HD].reshape(H, HD, HD)

time: 284 us -> 699 us (2.46)
  waiting for transfers between devices: 188 us -> 575 us
  starting transfers between devices: 15.5 us -> 45.3 us
  between operations: 14.2 us -> 0.9 us
  other arithmetic: 24.4 us -> 36.2 us
    ppermute x0 -> x4, waiting for transfers between devices: none -> 550 us  [local(): lax.ppermute(summed, 'ctx', [(dev, dev ^ hop) for dev in range(16)])]
    psum x1 -> x0, waiting for transfers between devices: 162 us -> none  [local(): summed = lax.psum(grads, 'ctx')]
    ppermute x0 -> x4, starting transfers between devices: none -> 29.8 us  [local(): lax.ppermute(summed, 'ctx', [(dev, dev ^ hop) for dev in range(16)])]
    add x0 -> x3, other arithmetic: none -> 10.2 us  [local(): summed + lax.ppermute(summed, 'ctx', [(dev, dev ^ hop) for dev in range(1...]
  transfers between devices with their start and end apart: 5 -> 8, of which waited for: 2 -> 5; matrix products, arithmetic and copies ran while one was open for 6% -> 3% of each run, Pallas kernels for 0% -> 0%
where the time goes in v1:
time: 699 us; the launch traced here: 698 us
  waiting for transfers between devices  575 us (82%)
  starting transfers between devices  45.3 us (6%)
  other arithmetic  36.2 us (5%)
  matrix products  26.9 us (4%)
  local copies, waits for them, and re-layouts  13.7 us (2%)
    ppermute x4, waiting for transfers between devices, local(): lax.ppermute(summed, 'ctx', [(dev, dev ^ hop) for dev in range(16)])  550 us
    ppermute x4, starting transfers between devices, local(): lax.ppermute(summed, 'ctx', [(dev, dev ^ hop) for dev in range(16)])  29.8 us
    ppermute x4, waiting for transfers between devices, passed_along(): lax.ppermute(value, axis, [(source, source + steps) for source in range(l...  25.5 us
    ppermute x4, starting transfers between devices, passed_along(): lax.ppermute(value, axis, [(source, source + steps) for source in range(l...  15.5 us
  transfers between devices with their start and end apart: 8, of which 5 were waited for; matrix products, arithmetic and copies ran while one was open for 3% of the time, Pallas kernels for 0%

profile of v1, /device:TPU:0, one launch (start us, length us, event | category | flops | bytes accessed | tf_op | source)
XLA Modules:
  0.0 698.3 jit_solution(16202132383406210350)
XLA Ops:
  2.1 5.9 collective-permute-start.2
  8.0 2.4 collective-permute-start.3
  10.4 2.9 collective-permute-start
  13.4 4.2 collective-permute-start.1
  27.7 25.4 %collective-permute-done = bf16[512,1024]{1,0:T(8,128)(2,1)} collective-permute-done((bf16[512,1024]{1,0:T(8,128)(2,1)}, bf16[512,1024]{1,0:T(8,128)(2,1)}, u32[]{:S(2)}, u32[]{:S(2)}) %collective-permute-start) | collective-permute-done | bytes 1048608 | tf_op jit(solution)/shard_map/ppermute | solution.py:15
  53.1 3.1 pad_maximum_fusion.1
  56.2 4.7 copy.88
  62.9 2.4 fusion.31
  65.3 2.2 fusion.58
  68.0 7.7 %fusion.26 = bf16[2,512,512]{2,1,0:T(8,128)(2,1)} fusion(bf16[1536,2,512]{0,2,1:T(8,128)(2,1)} %bitcast.142, f32[2,512]{1,0:T(2,128)S(1)} %fusion.58, f32[2,1536,512]{2,1,0:T(8,128)} %copy-done.10, pred[512,1536]{0,1:T(8,128)(4,1)} %fusion.7), kind=kOutput, calls=%fused_computation.53 | convolution fusion | flops 1619003904 | bytes 11276288 | tf_op jit(solution)/shard_map/hqk,khd->qhd/dot_general | solution.py:64
  82.4 21.5 %collective-permute-start.4 = (f32[3072,512]{1,0:T(8,128)S(1)}, f32[3072,512]{1,0:T(8,128)S(1)}, u32[]{:S(2)}, u32[]{:S(2)}) collective-permute-start(f32[3072,512]{1,0:T(8,128)S(1)} %pad_maximum_fusion), channel_id=1, source_target_pairs={{0,1},{1,0},{2,3},{3,2},{4,5},{5,4},{6,7},{7,6},{8,9},{9,8},{10,11... | collective-permute-start | bytes 18874376 | tf_op jit(solution)/shard_map/ppermute | solution.py:92
  103.9 9.8 %collective-permute-done.4 = f32[3072,512]{1,0:T(8,128)S(1)} collective-permute-done((f32[3072,512]{1,0:T(8,128)S(1)}, f32[3072,512]{1,0:T(8,128)S(1)}, u32[]{:S(2)}, u32[]{:S(2)}) %collective-permute-start.4) | collective-permute-done | bytes 6291488 | tf_op jit(solution)/shard_map/ppermute | solution.py:92
  115.3 2.8 collective-permute-start.5
  118.1 135.9 %collective-permute-done.5 = f32[3072,512]{1,0:T(8,128)} collective-permute-done((f32[3072,512]{1,0:T(8,128)S(1)}, f32[3072,512]{1,0:T(8,128)}, u32[]{:S(2)}, u32[]{:S(2)}) %collective-permute-start.5) | collective-permute-done | bytes 6291488 | tf_op jit(solution)/shard_map/ppermute | solution.py:92
  254.1 4.3 add.99
  258.4 2.8 collective-permute-start.6
  261.2 135.0 %collective-permute-done.6 = f32[3072,512]{1,0:T(8,128)S(1)} collective-permute-done((f32[3072,512]{1,0:T(8,128)S(1)}, f32[3072,512]{1,0:T(8,128)S(1)}, u32[]{:S(2)}, u32[]{:S(2)}) %collective-permute-start.6) | collective-permute-done | bytes 6291488 | tf_op jit(solution)/shard_map/ppermute | solution.py:92
  396.1 4.2 add.100
  400.4 2.8 collective-permute-start.7
  403.4 269.1 %collective-permute-done.7 = f32[3072,512]{1,0:T(8,128)} collective-permute-done((f32[3072,512]{1,0:T(8,128)}, f32[3072,512]{1,0:T(8,128)}, u32[]{:S(2)}, u32[]{:S(2)}) %collective-permute-start.7) | collective-permute-done | bytes 6291488 | tf_op jit(solution)/shard_map/ppermute | solution.py:92
  672.5 5.8 fusion.1
  678.4 8.0 %multiply_convert_fusion = bf16[3072,512]{1,0:T(8,128)(2,1)S(1)} fusion(f32[3072]{0:T(1024)S(1)} %rsqrt_multiply_fusion, f32[3072,512]{1,0:T(8,128)} %add.100, f32[3072,512]{1,0:T(8,128)} %collective-permute-done.7, bf16[1024,512]{1,0:T(8,128)(2,1)S(1)} %copy-done.1, bf16[1024,512]{1,0:T(8,128)(2,1)S(1)} %copy-done.5, bf16[1024,512]{1,0:T(8,128)(2,1)S(1)} %copy-done.7), kind=kLoop, calls=%fused_computation.6 | loop fusion | flops 15728640 | bytes 18886656 | tf_op jit(solution)/shard_map/convert_element_type | solution.py:31
  690.0 5.3 fusion.11
  695.3 2.3 copy.105
  (62 shorter events, 26.8 us)
Async XLA Ops:
  2.1 58.8 %collective-permute-start.2 = (bf16[512,1024]{0,1:T(8,128)(2,1)S(1)}, bf16[512,1024]{0,1:T(8,128)(2,1)}, u32[]{:S(2)}, u32[]{:S(2)}) collective-permute-start(bf16[512,1024]{0,1:T(8,128)(2,1)S(1)} %copy.89), channel_id=1, source_target_pairs={{0,2},{1,3},{2,4},{3,5},{4,6},{5,7},{6,8},{7,9},{8,10},{9,11},{10,... | collective-permute-start | bytes 3145736 | tf_op jit(solution)/shard_map/ppermute | solution.py:15
  8.0 52.9 %collective-permute-start.3 = (bf16[512,1024]{0,1:T(8,128)(2,1)S(1)}, bf16[512,1024]{0,1:T(8,128)(2,1)}, u32[]{:S(2)}, u32[]{:S(2)}) collective-permute-start(bf16[512,1024]{0,1:T(8,128)(2,1)S(1)} %copy.89), channel_id=1, source_target_pairs={{0,1},{1,2},{2,3},{3,4},{4,5},{5,6},{6,7},{7,8},{8,9},{9,10},{10,1... | collective-permute-start | bytes 3145736 | tf_op jit(solution)/shard_map/ppermute | solution.py:15
  10.4 42.7 %collective-permute-start = (bf16[512,1024]{1,0:T(8,128)(2,1)}, bf16[512,1024]{1,0:T(8,128)(2,1)}, u32[]{:S(2)}, u32[]{:S(2)}) collective-permute-start(bf16[512,1024]{1,0:T(8,128)(2,1)} %param.9), channel_id=1, source_target_pairs={{0,2},{1,3},{2,4},{3,5},{4,6},{5,7},{6,8},{7,9},{8,10},{9,11},{10,... | collective-permute-start | bytes 3145736 | tf_op jit(solution)/shard_map/ppermute | solution.py:15
  13.4 39.8 %collective-permute-start.1 = (bf16[512,1024]{1,0:T(8,128)(2,1)}, bf16[512,1024]{1,0:T(8,128)(2,1)}, u32[]{:S(2)}, u32[]{:S(2)}) collective-permute-start(bf16[512,1024]{1,0:T(8,128)(2,1)} %param.9), channel_id=1, source_target_pairs={{0,1},{1,2},{2,3},{3,4},{4,5},{5,6},{6,7},{7,8},{8,9},{9,10},{10,1... | collective-permute-start | bytes 3145736 | tf_op jit(solution)/shard_map/ppermute | solution.py:15
  17.9 3.6 copy-start.6
  19.5 4.1 copy-start.4
  21.4 4.3 copy-start.8
  23.6 2.1 copy-start.16
  23.6 29.5 %copy-start.14 = (bf16[512,1024]{1,0:T(8,128)(2,1)S(1)}, bf16[512,1024]{1,0:T(8,128)(2,1)}, u32[]{:S(2)}) copy-start(bf16[512,1024]{1,0:T(8,128)(2,1)} %param.9) | copy-start | bytes 3145732
  60.9 1.9 copy-start.2
  62.9 2.4 copy-start.15
  65.3 2.7 copy-start.10
  68.0 7.8 %copy-start = (bf16[1024,512]{1,0:T(8,128)(2,1)S(1)}, bf16[1024,512]{1,0:T(8,128)(2,1)}, u32[]{:S(2)}) copy-start(bf16[1024,512]{1,0:T(8,128)(2,1)} %param.13) | copy-start | bytes 3145732
  75.7 2.1 copy-start.9
  75.7 2.2 copy-start.11
  77.9 1.6 copy-start.12
  82.4 31.3 %collective-permute-start.4 = (f32[3072,512]{1,0:T(8,128)S(1)}, f32[3072,512]{1,0:T(8,128)S(1)}, u32[]{:S(2)}, u32[]{:S(2)}) collective-permute-start(f32[3072,512]{1,0:T(8,128)S(1)} %pad_maximum_fusion), channel_id=1, source_target_pairs={{0,1},{1,0},{2,3},{3,2},{4,5},{5,4},{6,7},{7,6},{8,9},{9,8},{10,11... | collective-permute-start | bytes 18874376 | tf_op jit(solution)/shard_map/ppermute | solution.py:92
  115.3 138.7 %collective-permute-start.5 = (f32[3072,512]{1,0:T(8,128)S(1)}, f32[3072,512]{1,0:T(8,128)}, u32[]{:S(2)}, u32[]{:S(2)}) collective-permute-start(f32[3072,512]{1,0:T(8,128)S(1)} %fusion.56), channel_id=1, source_target_pairs={{0,2},{1,3},{2,0},{3,1},{4,6},{5,7},{6,4},{7,5},{8,10},{9,11},{10,... | collective-permute-start | bytes 18874376 | tf_op jit(solution)/shard_map/ppermute | solution.py:92
  258.4 137.7 %collective-permute-start.6 = (f32[3072,512]{1,0:T(8,128)S(1)}, f32[3072,512]{1,0:T(8,128)S(1)}, u32[]{:S(2)}, u32[]{:S(2)}) collective-permute-start(f32[3072,512]{1,0:T(8,128)S(1)} %add.99), channel_id=1, source_target_pairs={{0,4},{1,5},{2,6},{3,7},{4,0},{5,1},{6,2},{7,3},{8,12},{9,13},{10,... | collective-permute-start | bytes 18874376 | tf_op jit(solution)/shard_map/ppermute | solution.py:92
  400.4 272.1 %collective-permute-start.7 = (f32[3072,512]{1,0:T(8,128)}, f32[3072,512]{1,0:T(8,128)}, u32[]{:S(2)}, u32[]{:S(2)}) collective-permute-start(f32[3072,512]{1,0:T(8,128)} %add.100), channel_id=1, source_target_pairs={{0,8},{1,9},{2,10},{3,11},{4,12},{5,13},{6,14},{7,15},{8,0},{9,1},... | collective-permute-start | bytes 18874376 | tf_op jit(solution)/shard_map/ppermute | solution.py:92
  403.4 275.0 %copy-start.1 = (bf16[1024,512]{1,0:T(8,128)(2,1)S(1)}, bf16[1024,512]{1,0:T(8,128)(2,1)}, u32[]{:S(2)}) copy-start(bf16[1024,512]{1,0:T(8,128)(2,1)} %param.13) | copy-start | bytes 3145732
  403.4 275.0 %copy-start.5 = (bf16[1024,512]{1,0:T(8,128)(2,1)S(1)}, bf16[1024,512]{1,0:T(8,128)(2,1)}, u32[]{:S(2)}) copy-start(bf16[1024,512]{1,0:T(8,128)(2,1)} %param.12) | copy-start | bytes 3145732
  403.4 275.0 %copy-start.7 = (bf16[1024,512]{1,0:T(8,128)(2,1)S(1)}, bf16[1024,512]{1,0:T(8,128)(2,1)}, u32[]{:S(2)}) copy-start(bf16[1024,512]{1,0:T(8,128)(2,1)} %param.11) | copy-start | bytes 3145732
  686.4 1.5 copy-start.3
  (1 other events, 1.2 us)
